TPU v7x, 32 devices: a whole 2x2x4 slice. The times are simulated.
32 devices in a mesh: expert: 4 (over x, core), hidden: 8 (over z, y).
Axes of the slice: x: 2, y: 2, z: 4, core: 2. Of those that a mesh axis runs over, the one named last changes fastest.
Arguments:
- tokens: bfloat16 [128, 6144], P(('expert', 'hidden')), may hold values from -33 to 33
- norm_gain: float32 [6144], replicated, may hold values from 0.1 to 1.9
- gate_weight: bfloat16 [4, 6144, 8192], P('expert', None, 'hidden'), may hold values from -0.078125 to 0.078125
- up_weight: bfloat16 [4, 6144, 8192], P('expert', None, 'hidden'), may hold values from -0.078125 to 0.078125
- down_weight: bfloat16 [4, 8192, 6144], P('expert', 'hidden'), may hold values from -0.09375 to 0.09375
- expert_ids: int32 [128, 2], P('expert'), may hold values from 0 to 3, all different within a row; in each aligned block of 4 rows (0 to 3, 4 to 7, ...) at most 2 rows name the same one
- route_weight: float32 [128, 2], P('expert'), may hold values from 0.2 to 1
Outputs:
- settled_state: bfloat16 [128, 6144], P(('expert', 'hidden'))
Inputs may be any that keep to these rules, and one draw needn't show every extreme that they name: `expert_ids`: in each aligned block of 4 rows (the tokens of one device) the two ids of a row differ and no expert is named more than 2 times; some expert is named exactly 2 times.
All inputs are finite; a program needn't handle non-finite values.
Results may differ from a plain program's by a relative error of at most 0.0085.
Values may be sent and summed in bfloat16 or wider, within the bound.
A program may use at most 64 MiB of HBM per device.

v0:
```python
import jax
import jax.numpy as jnp
from jax import lax
from jax.sharding import PartitionSpec as P

ITERS = 2
EPSILON = 1e-05
NUDGE = 0.5


def rms_norm(values, norm_gain):
    widened = values.astype(jnp.float32)
    mean_square = jnp.mean(widened * widened, axis=-1, keepdims=True)
    return (widened * lax.rsqrt(mean_square + EPSILON) * norm_gain).astype(jnp.bfloat16)


def slot_table(id_blocks, experts, capacity):
    groups = id_blocks.shape[0]
    tok_count = id_blocks.shape[1]
    flat_ids = id_blocks.reshape(groups, tok_count * 2)
    expert_range = jnp.arange(experts, dtype=jnp.int32)
    one_hot = (flat_ids[:, :, None] == expert_range[None, None, :]).astype(jnp.int32)
    before = jnp.cumsum(one_hot, axis=1) - one_hot
    within = jnp.sum(before * one_hot, axis=2)
    return (flat_ids * capacity + within).reshape(groups, tok_count, 2)


def dispatch(token_block, slots, slot_count):
    groups = token_block.shape[0]
    tok_count = token_block.shape[1]
    width = token_block.shape[2]
    token_index = jnp.broadcast_to(
        jnp.arange(tok_count, dtype=jnp.int32)[None, :, None], slots.shape
    )
    group_index = jnp.broadcast_to(jnp.arange(groups, dtype=jnp.int32)[:, None, None], slots.shape)
    source = (
        jnp.full((groups, slot_count), tok_count, jnp.int32).at[group_index, slots].set(token_index)
    )
    padded = jnp.concatenate(
        [token_block, jnp.zeros((groups, 1, width), token_block.dtype)], axis=1
    )
    return jax.vmap(lambda table_rows, chosen: jnp.take(table_rows, chosen, axis=0))(padded, source)


def expert_partial(inputs, gate_weight, up_weight, down_weight):
    gate_value = jnp.dot(inputs, gate_weight[0], preferred_element_type=jnp.float32)
    up_value = jnp.dot(inputs, up_weight[0], preferred_element_type=jnp.float32)
    hidden_units = (jax.nn.silu(gate_value) * up_value).astype(jnp.bfloat16)
    return jnp.dot(hidden_units, down_weight[0], preferred_element_type=jnp.float32)


def on_device(tokens, norm_gain, gate_weight, up_weight, down_weight, expert_ids, route_weight):
    experts = lax.axis_size("expert")
    tok_count = tokens.shape[0]
    capacity = tok_count // 2
    slot_count = experts * capacity
    position = lax.axis_index("hidden")
    own_ids = lax.dynamic_slice_in_dim(expert_ids, position * tok_count, tok_count, 0)
    own_weights = lax.dynamic_slice_in_dim(route_weight, position * tok_count, tok_count, 0)
    own_slots = slot_table(own_ids[None], experts, capacity)[0]
    state = tokens
    for iteration in range(ITERS):
        normed = rms_norm(state, norm_gain)
        outgoing = dispatch(normed[None], own_slots[None], slot_count)[0]
        arrived = lax.all_to_all(outgoing, "expert", split_axis=0, concat_axis=0, tiled=True)
        gathered = lax.all_gather(arrived, "hidden", axis=0, tiled=True)
        partials = expert_partial(gathered, gate_weight, up_weight, down_weight)
        summed = lax.psum_scatter(
            partials.astype(jnp.bfloat16), "hidden", scatter_dimension=0, tiled=True
        )
        returned = lax.all_to_all(summed, "expert", split_axis=0, concat_axis=0, tiled=True)
        first = (
            jnp.take(returned, own_slots[:, 0], axis=0).astype(jnp.float32) * own_weights[:, 0:1]
        )
        second = (
            jnp.take(returned, own_slots[:, 1], axis=0).astype(jnp.float32) * own_weights[:, 1:2]
        )
        mixed = first + second
        state = (
            NUDGE * state.astype(jnp.float32) + NUDGE * (tokens.astype(jnp.float32) + mixed)
        ).astype(jnp.bfloat16)
    return state


def solution(mesh):
    placed = (
        P(("expert", "hidden"), None),
        P(),
        P("expert", None, "hidden"),
        P("expert", None, "hidden"),
        P("expert", "hidden", None),
        P("expert", None),
        P("expert", None),
    )
    return jax.shard_map(
        on_device,
        mesh=mesh,
        in_specs=placed,
        out_specs=P(("expert", "hidden"), None),
        check_vma=False,
    )
```

profile of v0, /device:TPU:0, one launch (start us, length us, event | category | flops | bytes accessed | tf_op | source)
XLA Modules:
  0.0 285.9 jit_solution(7350800166975226673)
XLA Ops:
  6.5 0.7 copy-done
  7.3 0.1 copy.20
  7.5 0.2 reduce_window_sum.11
  7.8 0.1 copy.17
  7.9 0.1 copy.19
  8.2 0.6 scatter_custom_fusion
  8.8 1.0 fusion.51
  9.8 0.9 fusion.56
  10.7 0.8 gather_fusion
  11.7 8.3 %all_to_all.48 = bf16[4,2,6144]{2,1,0:T(2,128)(2,1)S(1)} all-to-all(bf16[4,2,6144]{2,1,0:T(2,128)(2,1)S(1)} %all_to_all.32), channel_id=1, replica_groups=mesh['expert'=4,'hidden'=8] {'expert'}, dimensions={0} | all-to-all | bytes 196608 | tf_op jit(solution)/shard_map/all_to_all | solution.py:65
  20.1 32.4 %all_gather.6 = bf16[64,6144]{1,0:T(8,128)(2,1)S(1)} all-gather(bf16[8,6144]{1,0:T(8,128)(2,1)S(1)} %all_to_all.34), channel_id=1, replica_groups=mesh['expert'=4,'hidden'=8] {'hidden'}, dimensions={0}, use_global_device_ids=true | all-gather | bytes 884736 | tf_op jit(solution)/shard_map/all_gather | solution.py:66
  52.5 6.9 %fusion.10 = f32[64,1024]{1,0:T(8,128)S(1)} fusion(bf16[64,6144]{1,0:T(8,128)(2,1)S(1)} %all_gather.6, bf16[1,6144,1024]{2,1,0:T(8,128)(2,1)} %param.13), kind=kOutput, calls=%fused_computation.17 | convolution fusion | flops 805306368 | bytes 13631488 | tf_op jit(solution)/shard_map/dot_general | solution.py:46
  59.5 13.6 %fusion.12 = bf16[64,6144]{1,0:T(8,128)(2,1)} fusion(bf16[1,1024,6144]{2,1,0:T(8,128)(2,1)} %param.15, bf16[64,6144]{1,0:T(8,128)(2,1)S(1)} %all_gather.6, bf16[1,6144,1024]{2,1,0:T(8,128)(2,1)} %param.14, f32[64,1024]{1,0:T(8,128)S(1)} %fusion.10), kind=kOutput, calls=%fused_computation.19 | convolution fusion | flops 1611399168 | bytes 27000832 | tf_op jit(solution)/shard_map/dot_general | solution.py:49
  73.2 0.2 slice_reduce_fusion.1
  73.4 63.1 %reduce-scatter.3.cloned.1.call-done = bf16[8,6144]{1,0:T(8,128)(2,1)} async-done(((bf16[64,6144]{1,0:T(8,128)(2,1)}), bf16[8,6144]{1,0:T(8,128)(2,1)}) %reduce-scatter.3.cloned.1.call-update) | async-done | bytes 98320 | tf_op jit(solution)/shard_map/reduce_scatter | solution.py:68
  136.5 1.6 all_to_all.35
  138.1 3.3 %all-to-all-start.1 = ((bf16[4,2,6144]{2,1,0:T(2,128)(2,1)}), bf16[4,2,6144]{2,1,0:T(2,128)(2,1)S(1)}, u32[]{:S(2)}, u32[]{:S(2)}) async-start(bf16[4,2,6144]{2,1,0:T(2,128)(2,1)} %all_to_all.35), calls=%async_computation.2 | async-start | bytes 196608 | tf_op jit(solution)/shard_map/all_to_all | solution.py:71
  141.5 4.2 %all-to-all-done.1 = bf16[4,2,6144]{2,1,0:T(2,128)(2,1)S(1)} async-done(((bf16[4,2,6144]{2,1,0:T(2,128)(2,1)}), bf16[4,2,6144]{2,1,0:T(2,128)(2,1)S(1)}, u32[]{:S(2)}, u32[]{:S(2)}) %all-to-all-start.1) | async-done | bytes 98336 | tf_op jit(solution)/shard_map/all_to_all | solution.py:71
  145.7 0.6 gather_fusion.2
  146.3 0.6 gather_fusion.1
  146.9 0.3 fusion.46
  147.3 0.8 gather_fusion.3
  148.3 6.7 %all_to_all.49 = bf16[4,2,6144]{2,1,0:T(2,128)(2,1)S(1)} all-to-all(bf16[4,2,6144]{2,1,0:T(2,128)(2,1)S(1)} %all_to_all.38), channel_id=1, replica_groups=mesh['expert'=4,'hidden'=8] {'expert'}, dimensions={0} | all-to-all | bytes 196608 | tf_op jit(solution)/shard_map/all_to_all | solution.py:65
  155.1 32.3 %all_gather.7 = bf16[64,6144]{1,0:T(8,128)(2,1)S(1)} all-gather(bf16[8,6144]{1,0:T(8,128)(2,1)S(1)} %all_to_all.40), channel_id=1, replica_groups=mesh['expert'=4,'hidden'=8] {'hidden'}, dimensions={0}, use_global_device_ids=true | all-gather | bytes 884736 | tf_op jit(solution)/shard_map/all_gather | solution.py:66
  187.3 6.9 %fusion.8 = f32[64,1024]{1,0:T(8,128)S(1)} fusion(bf16[64,6144]{1,0:T(8,128)(2,1)S(1)} %all_gather.7, bf16[1,6144,1024]{2,1,0:T(8,128)(2,1)} %param.13), kind=kOutput, calls=%fused_computation.15 | convolution fusion | flops 805306368 | bytes 13631488 | tf_op jit(solution)/shard_map/dot_general | solution.py:46
  194.2 13.6 %fusion.15 = bf16[64,6144]{1,0:T(8,128)(2,1)} fusion(bf16[1,1024,6144]{2,1,0:T(8,128)(2,1)} %param.15, bf16[64,6144]{1,0:T(8,128)(2,1)S(1)} %all_gather.7, bf16[1,6144,1024]{2,1,0:T(8,128)(2,1)} %param.14, f32[64,1024]{1,0:T(8,128)S(1)} %fusion.8), kind=kOutput, calls=%fused_computation.20 | convolution fusion | flops 1611399168 | bytes 27000832 | tf_op jit(solution)/shard_map/dot_general | solution.py:49
  207.8 61.5 %reduce-scatter.5.cloned.1.call-done = bf16[8,6144]{1,0:T(8,128)(2,1)} async-done(((bf16[64,6144]{1,0:T(8,128)(2,1)}), bf16[8,6144]{1,0:T(8,128)(2,1)}) %reduce-scatter.5.cloned.1.call-update) | async-done | bytes 98320 | tf_op jit(solution)/shard_map/reduce_scatter | solution.py:68
  269.3 1.0 all_to_all.41
  270.3 6.8 %all_to_all.50 = bf16[4,2,6144]{2,1,0:T(2,128)(2,1)S(1)} all-to-all(bf16[4,2,6144]{2,1,0:T(2,128)(2,1)S(1)} %all_to_all.41), channel_id=1, replica_groups=mesh['expert'=4,'hidden'=8] {'expert'}, dimensions={0} | all-to-all | bytes 196608 | tf_op jit(solution)/shard_map/all_to_all | solution.py:71
  277.1 0.6 gather_fusion.5
  277.7 0.6 gather_fusion.4
  278.3 0.8 fusion.50
  (45 shorter events, 1.3 us)
Async XLA Ops:
  6.5 0.7 copy-start
  6.5 130.0 %reduce-scatter.3.cloned.1.call-start = ((), (), s32[]{:S(2)}) async-start(), calls=%async_computation.6 | async-start | bytes 884736 | tf_op jit(solution)/shard_map/reduce_scatter | solution.py:68
  59.4 13.7 %copy-start.3 = (f32[32,2]{0,1:T(2,128)S(1)}, f32[32,2]{0,1:T(2,128)}, u32[]{:S(2)}) copy-start(f32[32,2]{0,1:T(2,128)} %param.17) | copy-start | bytes 772
  59.4 87.5 %copy-start.1 = (bf16[4,6144]{1,0:T(4,128)(2,1)S(1)}, bf16[4,6144]{1,0:T(4,128)(2,1)}, u32[]{:S(2)}) copy-start(bf16[4,6144]{1,0:T(4,128)(2,1)} %param.11) | copy-start | bytes 147460
  59.4 87.8 %copy-start.2 = (f32[6144]{0:T(1024)S(1)}, f32[6144]{0:T(1024)}, u32[]{:S(2)}) copy-start(f32[6144]{0:T(1024)} %param.12) | copy-start | bytes 73732
  138.1 7.6 %all-to-all-start.1 = ((bf16[4,2,6144]{2,1,0:T(2,128)(2,1)}), bf16[4,2,6144]{2,1,0:T(2,128)(2,1)S(1)}, u32[]{:S(2)}, u32[]{:S(2)}) async-start(bf16[4,2,6144]{2,1,0:T(2,128)(2,1)} %all_to_all.35), calls=%async_computation.2 | async-start | bytes 196608 | tf_op jit(solution)/shard_map/all_to_all | solution.py:71
  141.4 127.9 %reduce-scatter.5.cloned.1.call-start = ((), (), s32[]{:S(2)}) async-start(), calls=%async_computation.7 | async-start | bytes 884736 | tf_op jit(solution)/shard_map/reduce_scatter | solution.py:68
Sparse Core Ops, SparseCore 0:
  73.2 63.2 reduce-scatter.2
  207.9 61.2 reduce-scatter.4
where the time goes:
time: 286 us
  waiting for transfers between devices  129 us (45%)
  blocking collectives  86.4 us (30%)
  matrix products  40.9 us (14%)
  between operations  13.6 us (5%)
  local copies, waits for them, and re-layouts  9.26 us (3%)
  other arithmetic  3.46 us (1%)
  starting transfers between devices  3.35 us (1%)
    reduce_scatter x2, waiting for transfers between devices, on_device(): lax.psum_scatter(partials.astype(jnp.bfloat16), 'hidden', scatter_dimensi...  125 us
    all_gather x2, blocking collectives, on_device(): gathered = lax.all_gather(arrived, 'hidden', axis=0, tiled=True)  64.7 us
    dot_general x2, matrix products, expert_partial(): jnp.dot(hidden_units, down_weight[0], preferred_element_type=jnp.float32)  27.2 us
    all_to_all x2, blocking collectives, on_device(): lax.all_to_all(outgoing, 'expert', split_axis=0, concat_axis=0, tiled=True)  15 us
    dot_general x2, matrix products, expert_partial(): jnp.dot(inputs, gate_weight[0], preferred_element_type=jnp.float32)  13.8 us
    all_to_all x1, blocking collectives, on_device(): lax.all_to_all(summed, 'expert', split_axis=0, concat_axis=0, tiled=True)  6.77 us
  transfers between devices with their start and end apart: 3, of which 3 were waited for; matrix products, arithmetic and copies ran while one was open for 0% of the time, Pallas kernels for 0%

commit v1 on v0

--- a/solution.py
+++ b/solution.py
@@ -63,7 +63,9 @@
         normed = rms_norm(state, norm_gain)
         outgoing = dispatch(normed[None], own_slots[None], slot_count)[0]
         arrived = lax.all_to_all(outgoing, "expert", split_axis=0, concat_axis=0, tiled=True)
-        gathered = lax.all_gather(arrived, "hidden", axis=0, tiled=True)
+        gathered = jnp.concatenate(
+            lax.all_to_all(jnp.stack([arrived] * lax.axis_size("hidden")), "hidden", 0, 0), axis=0
+        )
         partials = expert_partial(gathered, gate_weight, up_weight, down_weight)
         summed = lax.psum_scatter(
             partials.astype(jnp.bfloat16), "hidden", scatter_dimension=0, tiled=True

time: 286 us -> 269 us (0.941)
  blocking collectives: 86.4 us -> 70.6 us
    all_gather x2 -> x0, blocking collectives: 64.7 us -> none  [on_device(): gathered = lax.all_gather(arrived, 'hidden', axis=0, tiled=True)]
    all_to_all x0 -> x2, blocking collectives: none -> 48.7 us  [on_device(): lax.all_to_all(jnp.stack([arrived] * lax.axis_size('hidden')), 'hidden',...]
where the time goes in v1:
time: 269 us
  waiting for transfers between devices  127 us (47%)
  blocking collectives  70.6 us (26%)
  matrix products  40.9 us (15%)
  between operations  13.6 us (5%)
  local copies, waits for them, and re-layouts  9.36 us (3%)
  other arithmetic  3.46 us (1%)
  starting transfers between devices  3.35 us (1%)
    reduce_scatter x2, waiting for transfers between devices, on_device(): lax.psum_scatter(partials.astype(jnp.bfloat16), 'hidden', scatter_dimensi...  123 us
    all_to_all x2, blocking collectives, on_device(): lax.all_to_all(jnp.stack([arrived] * lax.axis_size('hidden')), 'hidden',...  48.7 us
    dot_general x2, matrix products, expert_partial(): jnp.dot(hidden_units, down_weight[0], preferred_element_type=jnp.float32)  27.2 us
    all_to_all x2, blocking collectives, on_device(): lax.all_to_all(outgoing, 'expert', split_axis=0, concat_axis=0, tiled=True)  15 us
    dot_general x2, matrix products, expert_partial(): jnp.dot(inputs, gate_weight[0], preferred_element_type=jnp.float32)  13.8 us
    all_to_all x1, blocking collectives, on_device(): lax.all_to_all(summed, 'expert', split_axis=0, concat_axis=0, tiled=True)  6.84 us
  transfers between devices with their start and end apart: 3, of which 3 were waited for; matrix products, arithmetic and copies ran while one was open for 0% of the time, Pallas kernels for 0%

profile of v1, /device:TPU:0, one launch (start us, length us, event | category | flops | bytes accessed | tf_op | source)
XLA Modules:
  0.0 268.5 jit_solution(3975840039827679754)
XLA Ops:
  6.5 0.7 copy-done
  7.3 0.1 copy.20
  7.5 0.2 reduce_window_sum.11
  7.8 0.1 copy.17
  7.9 0.1 copy.19
  8.2 0.6 scatter_custom_fusion
  8.8 1.0 fusion.59
  9.8 0.9 fusion.64
  10.7 0.8 gather_fusion
  11.7 8.3 %all_to_all.52 = bf16[4,2,6144]{2,1,0:T(2,128)(2,1)S(1)} all-to-all(bf16[4,2,6144]{2,1,0:T(2,128)(2,1)S(1)} %all_to_all.34), channel_id=1, replica_groups=mesh['expert'=4,'hidden'=8] {'expert'}, dimensions={0} | all-to-all | bytes 196608 | tf_op jit(solution)/shard_map/all_to_all | solution.py:65
  20.2 25.5 %all_to_all.53 = bf16[8,8,6144]{2,1,0:T(8,128)(2,1)S(1)} all-to-all(bf16[8,8,6144]{2,1,0:T(8,128)(2,1)S(1)} %stack.9), channel_id=1, replica_groups=mesh['expert'=4,'hidden'=8] {'hidden'}, dimensions={0} | all-to-all | bytes 1572864 | tf_op jit(solution)/shard_map/all_to_all | solution.py:67
  45.7 6.9 %fusion.10 = f32[64,1024]{1,0:T(8,128)S(1)} fusion(bf16[1,6144,1024]{2,1,0:T(8,128)(2,1)} %param.13, bf16[8,8,6144]{2,1,0:T(8,128)(2,1)S(1)} %all_to_all.53), kind=kOutput, calls=%fused_computation.17 | convolution fusion | flops 805306368 | bytes 13631488 | tf_op jit(solution)/shard_map/dot_general | solution.py:46
  52.6 13.6 %fusion.12 = bf16[64,6144]{1,0:T(8,128)(2,1)} fusion(bf16[1,1024,6144]{2,1,0:T(8,128)(2,1)} %param.15, bf16[1,6144,1024]{2,1,0:T(8,128)(2,1)} %param.14, bf16[8,8,6144]{2,1,0:T(8,128)(2,1)S(1)} %all_to_all.53, f32[64,1024]{1,0:T(8,128)S(1)} %fusion.10), kind=kOutput, calls=%fused_computation.19 | convolution fusion | flops 1611399168 | bytes 27000832 | tf_op jit(solution)/shard_map/dot_general | solution.py:49
  66.3 0.2 slice_reduce_fusion.1
  66.5 61.3 %reduce-scatter.3.cloned.1.call-done = bf16[8,6144]{1,0:T(8,128)(2,1)} async-done(((bf16[64,6144]{1,0:T(8,128)(2,1)}), bf16[8,6144]{1,0:T(8,128)(2,1)}) %reduce-scatter.3.cloned.1.call-update) | async-done | bytes 98320 | tf_op jit(solution)/shard_map/reduce_scatter | solution.py:70
  127.9 1.6 all_to_all.37
  129.5 3.3 %all-to-all-start.2 = ((bf16[4,2,6144]{2,1,0:T(2,128)(2,1)}), bf16[4,2,6144]{2,1,0:T(2,128)(2,1)S(1)}, u32[]{:S(2)}, u32[]{:S(2)}) async-start(bf16[4,2,6144]{2,1,0:T(2,128)(2,1)} %all_to_all.37), calls=%async_computation.3 | async-start | bytes 196608 | tf_op jit(solution)/shard_map/all_to_all | solution.py:73
  132.9 4.2 %all-to-all-done.2 = bf16[4,2,6144]{2,1,0:T(2,128)(2,1)S(1)} async-done(((bf16[4,2,6144]{2,1,0:T(2,128)(2,1)}), bf16[4,2,6144]{2,1,0:T(2,128)(2,1)S(1)}, u32[]{:S(2)}, u32[]{:S(2)}) %all-to-all-start.2) | async-done | bytes 98336 | tf_op jit(solution)/shard_map/all_to_all | solution.py:73
  137.1 0.6 gather_fusion.2
  137.7 0.6 gather_fusion.1
  138.3 0.3 fusion.54
  138.7 0.8 gather_fusion.3
  139.7 6.7 %all_to_all.54 = bf16[4,2,6144]{2,1,0:T(2,128)(2,1)S(1)} all-to-all(bf16[4,2,6144]{2,1,0:T(2,128)(2,1)S(1)} %all_to_all.40), channel_id=1, replica_groups=mesh['expert'=4,'hidden'=8] {'expert'}, dimensions={0} | all-to-all | bytes 196608 | tf_op jit(solution)/shard_map/all_to_all | solution.py:65
  146.5 23.2 %all_to_all.55 = bf16[8,8,6144]{2,1,0:T(8,128)(2,1)S(1)} all-to-all(bf16[8,8,6144]{2,1,0:T(8,128)(2,1)S(1)} %stack.11), channel_id=1, replica_groups=mesh['expert'=4,'hidden'=8] {'hidden'}, dimensions={0} | all-to-all | bytes 1572864 | tf_op jit(solution)/shard_map/all_to_all | solution.py:67
  169.7 6.9 %fusion.8 = f32[64,1024]{1,0:T(8,128)S(1)} fusion(bf16[1,6144,1024]{2,1,0:T(8,128)(2,1)} %param.13, bf16[8,8,6144]{2,1,0:T(8,128)(2,1)S(1)} %all_to_all.55), kind=kOutput, calls=%fused_computation.15 | convolution fusion | flops 805306368 | bytes 13631488 | tf_op jit(solution)/shard_map/dot_general | solution.py:46
  176.6 13.6 %fusion.15 = bf16[64,6144]{1,0:T(8,128)(2,1)} fusion(bf16[1,1024,6144]{2,1,0:T(8,128)(2,1)} %param.15, bf16[1,6144,1024]{2,1,0:T(8,128)(2,1)} %param.14, bf16[8,8,6144]{2,1,0:T(8,128)(2,1)S(1)} %all_to_all.55, f32[64,1024]{1,0:T(8,128)S(1)} %fusion.8), kind=kOutput, calls=%fused_computation.20 | convolution fusion | flops 1611399168 | bytes 27000832 | tf_op jit(solution)/shard_map/dot_general | solution.py:49
  190.2 61.6 %reduce-scatter.5.cloned.1.call-done = bf16[8,6144]{1,0:T(8,128)(2,1)} async-done(((bf16[64,6144]{1,0:T(8,128)(2,1)}), bf16[8,6144]{1,0:T(8,128)(2,1)}) %reduce-scatter.5.cloned.1.call-update) | async-done | bytes 98320 | tf_op jit(solution)/shard_map/reduce_scatter | solution.py:70
  251.9 1.0 all_to_all.43
  252.8 6.8 %all_to_all.56 = bf16[4,2,6144]{2,1,0:T(2,128)(2,1)S(1)} all-to-all(bf16[4,2,6144]{2,1,0:T(2,128)(2,1)S(1)} %all_to_all.43), channel_id=1, replica_groups=mesh['expert'=4,'hidden'=8] {'expert'}, dimensions={0} | all-to-all | bytes 196608 | tf_op jit(solution)/shard_map/all_to_all | solution.py:73
  259.7 0.6 gather_fusion.5
  260.3 0.6 gather_fusion.4
  260.9 0.8 fusion.58
  (47 shorter events, 1.5 us)
Async XLA Ops:
  6.5 0.7 copy-start
  6.5 121.3 %reduce-scatter.3.cloned.1.call-start = ((), (), s32[]{:S(2)}) async-start(), calls=%async_computation.8 | async-start | bytes 884736 | tf_op jit(solution)/shard_map/reduce_scatter | solution.py:70
  52.6 13.7 %copy-start.3 = (f32[32,2]{0,1:T(2,128)S(1)}, f32[32,2]{0,1:T(2,128)}, u32[]{:S(2)}) copy-start(f32[32,2]{0,1:T(2,128)} %param.17) | copy-start | bytes 772
  52.6 85.7 %copy-start.1 = (bf16[4,6144]{1,0:T(4,128)(2,1)S(1)}, bf16[4,6144]{1,0:T(4,128)(2,1)}, u32[]{:S(2)}) copy-start(bf16[4,6144]{1,0:T(4,128)(2,1)} %param.11) | copy-start | bytes 147460
  52.6 86.0 %copy-start.2 = (f32[6144]{0:T(1024)S(1)}, f32[6144]{0:T(1024)}, u32[]{:S(2)}) copy-start(f32[6144]{0:T(1024)} %param.12) | copy-start | bytes 73732
  129.5 7.6 %all-to-all-start.2 = ((bf16[4,2,6144]{2,1,0:T(2,128)(2,1)}), bf16[4,2,6144]{2,1,0:T(2,128)(2,1)S(1)}, u32[]{:S(2)}, u32[]{:S(2)}) async-start(bf16[4,2,6144]{2,1,0:T(2,128)(2,1)} %all_to_all.37), calls=%async_computation.3 | async-start | bytes 196608 | tf_op jit(solution)/shard_map/all_to_all | solution.py:73
  132.8 119.1 %reduce-scatter.5.cloned.1.call-start = ((), (), s32[]{:S(2)}) async-start(), calls=%async_computation.9 | async-start | bytes 884736 | tf_op jit(solution)/shard_map/reduce_scatter | solution.py:70
Sparse Core Ops, SparseCore 0:
  66.3 61.4 reduce-scatter.2
  190.4 61.4 reduce-scatter.4
